TPU v7x, 256 devices: a whole 4x4x8 slice. The times are simulated.
256 devices in a mesh: dp: 64 (over z, y, x_hi), mp: 4 (over x_lo, core).
Axes of the slice: x: 4 (x_hi: 2, x_lo: 2; x = x_hi * 2 + x_lo), y: 4, z: 8, core: 2. Of those that a mesh axis runs over, the one named last changes fastest.
Arguments:
- streams: bfloat16 [16384, 4, 8192], P('dp', None, 'mp'), may hold values from -200 to 200
- branch_out: bfloat16 [16384, 8192], P('dp', 'mp'), may hold values from -6 to 6
- merge_weight: float32 [20, 4, 8192], P(None, None, ('mp', 'dp')), may hold values from -0.03125 to 0.03125
- next_weight: float32 [24, 4, 8192], P(None, None, ('mp', 'dp')), may hold values from -0.03125 to 0.03125
- blend_bias: float32 [44], replicated, may hold values from -3 to 3
- blend_scale: float32 [5], replicated, may hold values from 0.5 to 3
- norm_gain: float32 [8192], P('mp'), may hold values from 0.5 to 1.5
Outputs:
- streams_out: bfloat16 [16384, 4, 8192], P('dp', None, 'mp')
- branch_in: bfloat16 [16384, 8192], P('dp', 'mp')
- next_mix: float32 [16384, 20], P('dp')
All inputs are finite; a program needn't handle non-finite values.
Results may differ from a plain program's by a relative error of at most 0.001.
Values sent between devices are 32-bit elements; how exact they have to be, the bound alone decides.
A program may use at most 64 MiB of HBM per device.

v0:
```python
import jax
import jax.numpy as jnp
from jax import lax
from jax.sharding import PartitionSpec as P

D = 8192
STREAMS = 4
BALANCE_ROUNDS = 6
epsilon = 1e-06


def copy_for_each(x, axis):
    peers = lax.axis_size(axis)
    return lax.all_to_all(jnp.broadcast_to(x[None], (peers, *x.shape)), axis, 0, 0, tiled=True)


def of_everyone(x, axis):
    everything = copy_for_each(x, axis)
    return jnp.sum(everything, axis=0)


def turned_gather(arrays, axis, dims):
    turned = [jnp.moveaxis(a, dim, 0) for a, dim in zip(arrays, dims)]
    both = jnp.concatenate([t.reshape(len(t), -1) for t in turned], axis=1)
    filled, at, gathered = (lax.all_gather(both, axis, axis=0, tiled=True), 0, [])
    for t, dim in zip(turned, dims):
        section = filled[:, at : at + t[0].size].reshape(-1, *t.shape[1:])
        gathered.append(jnp.moveaxis(section, 0, dim))
        at += t[0].size
    return tuple(gathered)


def balance_normalize(balanced_matrix):
    for balance_round in range(BALANCE_ROUNDS):
        balanced_matrix = balanced_matrix / jnp.sum(balanced_matrix, axis=2, keepdims=True)
        balanced_matrix = balanced_matrix / jnp.sum(balanced_matrix, axis=1, keepdims=True)
    return balanced_matrix


def settle(columns, finish):
    summed = of_everyone(columns, "mp")
    result = finish(summed)
    return result


def first_coef(raw_sums, squares, blend_bias, blend_scale):
    rms_root = jnp.sqrt(squares / (STREAMS * D) + epsilon)
    score_logits = raw_sums / rms_root[:, None]
    post_mix = 2.0 * jax.nn.sigmoid(blend_scale[0] * score_logits[:, :4] + blend_bias[:4])
    residual_blend = balance_normalize(
        jnp.exp(
            blend_scale[1] * score_logits[:, 4:20].reshape(-1, 4, 4)
            + blend_bias[4:20].reshape(4, 4)
        )
    )
    return (post_mix, residual_blend)


def second_coef(raw_sums, squares, blend_bias, blend_scale):
    rms_root = jnp.sqrt(squares / (STREAMS * D) + epsilon)
    score_logits = raw_sums / rms_root[:, None]
    pre_next = jax.nn.sigmoid(blend_scale[2] * score_logits[:, :4] + blend_bias[20:24])
    post_next = 2.0 * jax.nn.sigmoid(blend_scale[3] * score_logits[:, 4:8] + blend_bias[24:28])
    residual_following = balance_normalize(
        jnp.exp(
            blend_scale[4] * score_logits[:, 8:24].reshape(-1, 4, 4)
            + blend_bias[28:44].reshape(4, 4)
        )
    )
    return (pre_next, post_next, residual_following)


def mix_streams(residual_blend, post_mix, streams, branch_out):
    branch_wide = branch_out.astype(jnp.float32)
    outputs = []
    for target in range(STREAMS):
        total = post_mix[:, target, None] * branch_wide
        for source in range(STREAMS):
            total = total + residual_blend[:, target, source, None] * streams[:, source, :].astype(
                jnp.float32
            )
        outputs.append(total)
    return jnp.stack(outputs, axis=1)


def unite(pre_next, mixed):
    total = pre_next[:, 0, None] * mixed[:, 0, :]
    for source in range(1, STREAMS):
        total = total + pre_next[:, source, None] * mixed[:, source, :]
    return total


def local(streams, branch_out, merge_weight, next_weight, blend_bias, blend_scale, norm_gain):
    merge_rows, next_rows = turned_gather((merge_weight, next_weight), "dp", (2, 2))
    highest = lax.Precision.HIGHEST
    raw_part = jnp.einsum(
        "tic,kic->tk", streams, merge_rows, precision=highest, preferred_element_type=jnp.float32
    )
    gram_part = jnp.einsum("tic,tjc->tij", streams, streams, preferred_element_type=jnp.float32)
    columns = jnp.concatenate([raw_part, jnp.trace(gram_part, axis1=1, axis2=2)[:, None]], axis=1)

    def finish_first(summed):
        post_mix, residual_blend = first_coef(
            summed[:, :20], summed[:, 20], blend_bias, blend_scale
        )
        return jnp.concatenate([post_mix, residual_blend.reshape(-1, 16)], axis=1)

    merge_coef = settle(columns, finish_first)
    post_mix = merge_coef[:, :4]
    residual_blend = merge_coef[:, 4:20].reshape(-1, 4, 4)
    mixed = mix_streams(residual_blend, post_mix, streams, branch_out)
    streams_out = mixed.astype(jnp.bfloat16)
    raw_next = jnp.einsum("tic,kic->tk", mixed, next_rows, precision=highest)
    extra_cols = jnp.sum(mixed * mixed, axis=(1, 2))[:, None]
    columns_next = jnp.concatenate([raw_next, extra_cols], axis=1)

    def finish_second(summed):
        squares = summed[:, 24]
        pre_next, post_next, residual_following = second_coef(
            summed[:, :24], squares, blend_bias, blend_scale
        )
        pieces = [pre_next, post_next, residual_following.reshape(-1, 16)]
        return jnp.concatenate(pieces, axis=1)

    next_coef = settle(columns_next, finish_second)
    pre_next = next_coef[:, :4]
    next_mix = next_coef[:, 4:24]
    united = unite(pre_next, mixed)
    united_sq = of_everyone(jnp.sum(united * united, axis=1), "mp")
    branch_in = (united / jnp.sqrt(united_sq / D + epsilon)[:, None] * norm_gain).astype(
        jnp.bfloat16
    )
    return (streams_out, branch_in, next_mix)


def solution(mesh):
    placed = (
        P("dp", None, "mp"),
        P("dp", "mp"),
        P(None, None, ("mp", "dp")),
        P(None, None, ("mp", "dp")),
        P(),
        P(),
        P("mp"),
    )
    return jax.shard_map(
        local,
        mesh=mesh,
        in_specs=placed,
        out_specs=(P("dp", None, "mp"), P("dp", "mp"), P("dp", None)),
        check_vma=False,
    )
```

profile of v0, /device:TPU:1, one launch (start us, length us, event | category | flops | bytes accessed | tf_op | source)
XLA Modules:
  0.0 209.4 jit_solution(10708887090275913820)
XLA Ops:
  7.2 0.8 copy.64
  8.1 0.9 copy.65
  9.7 0.8 fusion.84
  10.6 6.7 %copy.68 = bf16[256,4,2048]{2,0,1:T(8,128)(2,1)} copy(bf16[256,4,2048]{2,1,0:T(4,128)(2,1)} %param.7) | data formatting | bytes 8388608 | tf_op args[0]
  17.4 5.8 %fusion.28 = f32[256]{0:T(256)S(1)} fusion(bf16[256,4,2048]{2,1,0:T(4,128)(2,1)S(1)} %copy-done.4, pred[4,4]{1,0:T(4,128)(4,1)S(1)} %iota_compare_fusion), kind=kOutput, calls=%fused_computation.54 | convolution fusion | flops 16785152 | bytes 4195344 | tf_op jit(solution)/shard_map/tic,tjc->tij/dot_general | solution.py:99
  23.1 107.6 %all-gather.2.cloned.1.call-done = f32[2048,176]{1,0:T(8,128)} async-done(((f32[32,176]{1,0:T(8,128)}), f32[2048,176]{1,0:T(8,128)}) %all-gather.2.cloned.1.call-update) | async-done | bytes 1441808 | tf_op jit(solution)/shard_map/all_gather | solution.py:25
  130.7 1.2 slice-done
  132.5 9.7 %convolution_bitcast_fusion = f32[256,20]{0,1:T(8,128)S(1)} fusion(f32[2048,20,4]{0,2,1:T(4,128)S(1)} %reshape.126, bf16[256,4,2048]{2,1,0:T(4,128)(2,1)} %param.7), kind=kOutput, calls=%fused_computation.56 | convolution fusion | flops 503316480 | bytes 4870144 | tf_op jit(solution)/shard_map/tic,kic->tk/dot_general | solution.py:96
  142.8 7.7 %all-to-all-start = ((f32[4,256,21]{1,2,0:T(8,128)}), f32[4,256,21]{1,2,0:T(8,128)S(1)}, u32[]{:S(2)}, u32[]{:S(2)}) async-start(f32[4,256,21]{1,2,0:T(8,128)} %broadcast_in_dim.22), calls=%async_computation | async-start | bytes 196608 | tf_op jit(solution)/shard_map/all_to_all | solution.py:14
  151.2 1.9 slice.249
  153.4 1.1 reshape.127
  155.2 0.8 fusion.60
  156.4 4.0 %fusion.13 = (f32[256,2048]{1,0:T(8,128)S(1)}, f32[256,2048]{1,0:T(8,128)S(1)}) fusion(bf16[256,2048]{1,0:T(8,128)(2,1)S(1)} %copy-done.5, f32[256]{0:T(256)S(1)} %bitcast.153, f32[256]{0:T(256)S(1)} %bitcast.154, f32[256]{0:T(256)S(1)} %bitcast.155, f32[256]{0:T(256)S(1)} %bitcast.148, f32[256]{0:T(256)S(1)} %bitcast.158, bf16[256,4,2048]{2,0,1:T(8,128)(2,1)} %copy.68, ...), kind=kLoop, calls=%fused_computation.35 | loop fusion | flops 12058624 | bytes 9447424 | tf_op jit(solution)/shard_map/add | solution.py:79
  160.4 2.3 %fusion.21 = (f32[256,2048]{1,0:T(8,128)S(1)}, f32[256,2048]{1,0:T(8,128)S(1)}) fusion(bf16[256,2048]{1,0:T(8,128)(2,1)S(1)} %copy-done.5, f32[256]{0:T(256)S(1)} %bitcast.144, f32[256]{0:T(256)S(1)} %bitcast.145, f32[256]{0:T(256)S(1)} %bitcast.146, f32[256]{0:T(256)S(1)} %bitcast.147, f32[256]{0:T(256)S(1)} %bitcast.157, ...), kind=kLoop, calls=%fused_computation.43 | loop fusion | flops 12058624 | bytes 9447424 | tf_op jit(solution)/shard_map/add | solution.py:79
  162.7 0.9 multiply_reduce_fusion
  164.6 6.6 %fusion.29 = f32[256,24]{0,1:T(8,128)S(1)} fusion(f32[256,1,2048]{2,0,1:T(8,128)S(1)} %bitcast.128, f32[256,1,2048]{2,0,1:T(8,128)S(1)} %bitcast.125, f32[256,1,2048]{2,0,1:T(8,128)S(1)} %bitcast.122, f32[256,1,2048]{2,0,1:T(8,128)S(1)} %bitcast.119, f32[2048,24,4]{0,2,1:T(4,128)S(1)} %copy-done.6), kind=kOutput, calls=%fused_computation.55 | convolution fusion | flops 610271232 | bytes 9199616 | tf_op jit(solution)/shard_map/tic,kic->tk/dot_general | solution.py:113
  171.9 3.6 %all-to-all-start.1 = ((f32[4,256,25]{1,2,0:T(8,128)}), f32[4,256,25]{1,2,0:T(8,128)S(1)}, u32[]{:S(2)}, u32[]{:S(2)}) async-start(f32[4,256,25]{1,2,0:T(8,128)} %broadcast_in_dim.24), calls=%async_computation.1 | async-start | bytes 262144 | tf_op jit(solution)/shard_map/all_to_all | solution.py:14
  175.5 3.2 %fusion.27 = bf16[256,4,2048]{2,0,1:T(8,128)(2,1)S(1)} fusion(f32[256,1,2048]{2,0,1:T(8,128)} %bitcast.129, f32[256,1,2048]{2,0,1:T(8,128)} %bitcast.126, f32[256,1,2048]{2,0,1:T(8,128)} %bitcast.123, f32[256,1,2048]{2,0,1:T(8,128)S(1)} %bitcast.120), kind=kLoop, calls=%fused_computation.52 | loop fusion | flops 6291456 | bytes 12582912 | tf_op jit(solution)/shard_map/convert_element_type | solution.py:112
  178.8 5.3 %copy.76 = bf16[256,4,2048]{2,1,0:T(4,128)(2,1)} copy(bf16[256,4,2048]{2,0,1:T(8,128)(2,1)S(1)} %fusion.27) | data formatting | bytes 8388608
  184.1 1.3 fusion.49
  187.6 4.9 %multiply_reduce_fusion.1 = (f32[256]{0:T(256)S(1)}, f32[256,2048]{1,0:T(8,128)}) fusion(f32[256,2048]{1,0:T(8,128)} %copy-done.3, f32[256]{0:T(256)S(1)} %bitcast.161, f32[256,2048]{1,0:T(8,128)} %copy-done.2, f32[256]{0:T(256)S(1)} %bitcast.162, f32[256,2048]{1,0:T(8,128)} %copy-done.1, f32[256]{0:T(256)S(1)} %bitcast.163, ...), kind=kLoop, calls=%fused_computation.49 | loop fusion | flops 4718336 | bytes 10490880 | tf_op jit(solution)/shard_map/reduce_sum | solution.py:129
  193.1 3.5 %all-to-all-start.2 = ((f32[4,1,256]{2,1,0:T(1,128)}), f32[4,1,256]{2,1,0:T(1,128)S(1)}, u32[]{:S(2)}, u32[]{:S(2)}) async-start(f32[4,1,256]{2,1,0:T(1,128)} %broadcast_in_dim.25), calls=%async_computation.2 | async-start | bytes 8192 | tf_op jit(solution)/shard_map/all_to_all | solution.py:14
  197.2 2.5 %all-to-all-done.2 = f32[4,1,256]{2,1,0:T(1,128)S(1)} async-done(((f32[4,1,256]{2,1,0:T(1,128)}), f32[4,1,256]{2,1,0:T(1,128)S(1)}, u32[]{:S(2)}, u32[]{:S(2)}) %all-to-all-start.2) | async-done | bytes 4128 | tf_op jit(solution)/shard_map/all_to_all | solution.py:14
  199.7 2.9 %multiply_convert_fusion = bf16[256,2048]{1,0:T(8,128)(2,1)} fusion(f32[256,2048]{1,0:T(8,128)} %get-tuple-element.22, f32[2048]{0:T(1024)S(1)} %copy-done.9, f32[256]{0:T(256)S(1)} %add_sqrt_fusion), kind=kLoop, calls=%fused_computation.48 | loop fusion | flops 1572864 | bytes 3154944 | tf_op jit(solution)/shard_map/convert_element_type | solution.py:130
  (75 shorter events, 9.2 us)
Async XLA Ops:
  7.2 123.6 %all-gather.2.cloned.1.call-start = ((), (), s32[]{:S(2)}) async-start(), calls=%async_computation.3 | async-start | bytes 2129920 | tf_op jit(solution)/shard_map/all_gather | solution.py:25
  10.6 6.7 %copy-start.7 = (f32[44]{0:T(128)S(1)}, f32[44]{0:T(128)}, u32[]{:S(2)}) copy-start(f32[44]{0:T(128)} %param.11) | copy-start | bytes 532
  10.6 6.7 %copy-start.4 = (bf16[256,4,2048]{2,1,0:T(4,128)(2,1)S(1)}, bf16[256,4,2048]{2,1,0:T(4,128)(2,1)}, u32[]{:S(2)}) copy-start(bf16[256,4,2048]{2,1,0:T(4,128)(2,1)} %param.7) | copy-start | bytes 12582916
  130.7 1.2 slice-start
  132.5 18.1 %copy-start.8 = (f32[5]{0:T(128)S(1)}, f32[5]{0:T(128)}, u32[]{:S(2)}) copy-start(f32[5]{0:T(128)} %param.12) | copy-start | bytes 64
  142.8 11.7 %all-to-all-start = ((f32[4,256,21]{1,2,0:T(8,128)}), f32[4,256,21]{1,2,0:T(8,128)S(1)}, u32[]{:S(2)}, u32[]{:S(2)}) async-start(f32[4,256,21]{1,2,0:T(8,128)} %broadcast_in_dim.22), calls=%async_computation | async-start | bytes 196608 | tf_op jit(solution)/shard_map/all_to_all | solution.py:14
  153.4 2.9 %copy-start.5 = (bf16[256,2048]{1,0:T(8,128)(2,1)S(1)}, bf16[256,2048]{1,0:T(8,128)(2,1)}, u32[]{:S(2)}) copy-start(bf16[256,2048]{1,0:T(8,128)(2,1)} %param.8) | copy-start | bytes 3145732
  156.3 4.0 %copy-start = (bf16[256,4,2048]{2,0,1:T(8,128)(2,1)S(1)}, bf16[256,4,2048]{2,0,1:T(8,128)(2,1)}, u32[]{:S(2)}) copy-start(bf16[256,4,2048]{2,0,1:T(8,128)(2,1)} %copy.68) | copy-start | bytes 12582916
  160.3 3.2 %copy-start.1 = (f32[256,2048]{1,0:T(8,128)}, f32[256,2048]{1,0:T(8,128)S(1)}, u32[]{:S(2)}) copy-start(f32[256,2048]{1,0:T(8,128)S(1)} %get-tuple-element.26) | copy-start | bytes 6291460
  162.6 1.3 copy-start.2
  162.6 2.0 copy-start.3
  162.7 2.0 copy-start.6
  171.9 12.1 %all-to-all-start.1 = ((f32[4,256,25]{1,2,0:T(8,128)}), f32[4,256,25]{1,2,0:T(8,128)S(1)}, u32[]{:S(2)}, u32[]{:S(2)}) async-start(f32[4,256,25]{1,2,0:T(8,128)} %broadcast_in_dim.24), calls=%async_computation.1 | async-start | bytes 262144 | tf_op jit(solution)/shard_map/all_to_all | solution.py:14
  187.6 12.1 %copy-start.9 = (f32[2048]{0:T(1024)S(1)}, f32[2048]{0:T(1024)}, u32[]{:S(2)}) copy-start(f32[2048]{0:T(1024)} %param.13) | copy-start | bytes 24580
  193.1 6.6 %all-to-all-start.2 = ((f32[4,1,256]{2,1,0:T(1,128)}), f32[4,1,256]{2,1,0:T(1,128)S(1)}, u32[]{:S(2)}, u32[]{:S(2)}) async-start(f32[4,1,256]{2,1,0:T(1,128)} %broadcast_in_dim.25), calls=%async_computation.2 | async-start | bytes 8192 | tf_op jit(solution)/shard_map/all_to_all | solution.py:14
Sparse Core Ops, SparseCore 0:
  12.1 118.5 all-gather.1
where the time goes:
time: 210 us; the launch traced here: 209 us
  waiting for transfers between devices  110 us (52%)
  other arithmetic  24.6 us (12%)
  local copies, waits for them, and re-layouts  23.5 us (11%)
  matrix products  22.1 us (11%)
  starting transfers between devices  14.8 us (7%)
  between operations  14.4 us (7%)
    all_gather x1, waiting for transfers between devices, turned_gather(): lax.all_gather(both, axis, axis=0, tiled=True)  108 us
    all_to_all x3, starting transfers between devices, copy_for_each(): lax.all_to_all(jnp.broadcast_to(x[None], (peers, *x.shape)), axis, 0, 0,...  14.8 us
    unnamed x24, local copies, waits for them, and re-layouts  13 us
    dot_general x1, matrix products, local(): jnp.einsum('tic,kic->tk', streams, merge_rows, precision=highest, preferr...  9.68 us
    dot_general x1, matrix products, local(): raw_next = jnp.einsum('tic,kic->tk', mixed, next_rows, precision=highest)  6.63 us
    add x2, other arithmetic, mix_streams(): total + residual_blend[:, target, source, None] * streams[:, source, :].a...  6.25 us
    dot_general x1, matrix products, local(): jnp.einsum('tic,tjc->tij', streams, streams, preferred_element_type=jnp.f...  5.77 us
    reduce_sum x1, other arithmetic, local(): united_sq = of_everyone(jnp.sum(united * united, axis=1), 'mp')  4.89 us
  transfers between devices with their start and end apart: 4, of which 2 were waited for; matrix products, arithmetic and copies ran while one was open for 13% of the time, Pallas kernels for 0%

commit v1 on v0

--- a/solution.py
+++ b/solution.py
@@ -22,7 +22,13 @@
 def turned_gather(arrays, axis, dims):
     turned = [jnp.moveaxis(a, dim, 0) for a, dim in zip(arrays, dims)]
     both = jnp.concatenate([t.reshape(len(t), -1) for t in turned], axis=1)
-    filled, at, gathered = (lax.all_gather(both, axis, axis=0, tiled=True), 0, [])
+    filled, at, gathered = (
+        jnp.concatenate(
+            lax.all_to_all(jnp.stack([both] * lax.axis_size(axis)), axis, 0, 0), axis=0
+        ),
+        0,
+        [],
+    )
     for t, dim in zip(turned, dims):
         section = filled[:, at : at + t[0].size].reshape(-1, *t.shape[1:])
         gathered.append(jnp.moveaxis(section, 0, dim))

time: 210 us -> 142 us (0.68)
  waiting for transfers between devices: 110 us -> 39.5 us
  starting transfers between devices: 14.8 us -> 31 us
  between operations: 14.4 us -> 1 us
    all_gather x1 -> x0, waiting for transfers between devices: 108 us -> none  [turned_gather(): lax.all_gather(both, axis, axis=0, tiled=True)]
    all_to_all x0 -> x1, waiting for transfers between devices: none -> 36.1 us  [turned_gather(): lax.all_to_all(jnp.stack([both] * lax.axis_size(axis)), axis, 0, 0)]
    all_to_all x0 -> x1, starting transfers between devices: none -> 15.2 us  [turned_gather(): lax.all_to_all(jnp.stack([both] * lax.axis_size(axis)), axis, 0, 0)]
  transfers between devices with their start and end apart: 4 -> 4, of which waited for: 2 -> 3; matrix products, arithmetic and copies ran while one was open for 13% -> 17% of each run, Pallas kernels for 0% -> 0%
where the time goes in v1:
time: 142 us; the launch traced here: 141 us
  waiting for transfers between devices  39.5 us (28%)
  starting transfers between devices  31 us (22%)
  other arithmetic  24 us (17%)
  local copies, waits for them, and re-layouts  23.5 us (17%)
  matrix products  22.1 us (16%)
    all_to_all x1, waiting for transfers between devices, turned_gather(): lax.all_to_all(jnp.stack([both] * lax.axis_size(axis)), axis, 0, 0)  36.1 us
    all_to_all x3, starting transfers between devices, copy_for_each(): lax.all_to_all(jnp.broadcast_to(x[None], (peers, *x.shape)), axis, 0, 0,...  15.8 us
    all_to_all x1, starting transfers between devices, turned_gather(): lax.all_to_all(jnp.stack([both] * lax.axis_size(axis)), axis, 0, 0)  15.2 us
    unnamed x24, local copies, waits for them, and re-layouts  13 us
    dot_general x1, matrix products, local(): jnp.einsum('tic,kic->tk', streams, merge_rows, precision=highest, preferr...  9.68 us
    dot_general x1, matrix products, local(): raw_next = jnp.einsum('tic,kic->tk', mixed, next_rows, precision=highest)  6.63 us
    add x2, other arithmetic, mix_streams(): total + residual_blend[:, target, source, None] * streams[:, source, :].a...  6.26 us
    dot_general x1, matrix products, local(): jnp.einsum('tic,tjc->tij', streams, streams, preferred_element_type=jnp.f...  5.77 us
  transfers between devices with their start and end apart: 4, of which 3 were waited for; matrix products, arithmetic and copies ran while one was open for 17% of the time, Pallas kernels for 0%

profile of v1, /device:TPU:1, one launch (start us, length us, event | category | flops | bytes accessed | tf_op | source)
XLA Modules:
  0.0 141.1 jit_solution(6994239515330747055)
XLA Ops:
  1.5 0.9 copy.79
  2.4 1.6 %stack.12 = f32[64,32,176]{2,1,0:T(8,128)} broadcast(f32[32,176]{1,0:T(8,128)S(1)} %pad_maximum_fusion.4), dimensions={1,2} | broadcast | bytes 1464320 | tf_op jit(solution)/shard_map/stack | solution.py:27
  4.0 15.2 %all-to-all-start = ((f32[64,32,176]{2,1,0:T(8,128)}), f32[64,32,176]{2,1,0:T(8,128)S(1)}, u32[]{:S(2)}, u32[]{:S(2)}) async-start(f32[64,32,176]{2,1,0:T(8,128)} %stack.12), calls=%async_computation | async-start | bytes 4194304 | tf_op jit(solution)/shard_map/all_to_all | solution.py:27
  19.5 6.7 %copy.82 = bf16[256,4,2048]{2,0,1:T(8,128)(2,1)} copy(bf16[256,4,2048]{2,1,0:T(4,128)(2,1)} %param.7) | data formatting | bytes 8388608 | tf_op args[0]
  26.3 5.8 %fusion.28 = f32[256]{0:T(256)S(1)} fusion(bf16[256,4,2048]{2,1,0:T(4,128)(2,1)S(1)} %copy-done.4, pred[4,4]{1,0:T(4,128)(4,1)S(1)} %iota_compare_fusion), kind=kOutput, calls=%fused_computation.54 | convolution fusion | flops 16785152 | bytes 4195344 | tf_op jit(solution)/shard_map/tic,tjc->tij/dot_general | solution.py:105
  32.1 36.1 %all-to-all-done = f32[64,32,176]{2,1,0:T(8,128)S(1)} async-done(((f32[64,32,176]{2,1,0:T(8,128)}), f32[64,32,176]{2,1,0:T(8,128)S(1)}, u32[]{:S(2)}, u32[]{:S(2)}) %all-to-all-start) | async-done | bytes 1441824 | tf_op jit(solution)/shard_map/all_to_all | solution.py:27
  68.2 1.2 copy.80
  69.4 1.3 reshape.132
  70.7 9.7 %convolution_bitcast_fusion = f32[256,20]{0,1:T(8,128)S(1)} fusion(f32[2048,20,4]{0,2,1:T(4,128)S(1)} %reshape.132, bf16[256,4,2048]{2,1,0:T(4,128)(2,1)} %param.7), kind=kOutput, calls=%fused_computation.56 | convolution fusion | flops 503316480 | bytes 4870144 | tf_op jit(solution)/shard_map/tic,kic->tk/dot_general | solution.py:102
  81.0 8.1 %all-to-all-start.1 = ((f32[4,256,21]{1,2,0:T(8,128)}), f32[4,256,21]{1,2,0:T(8,128)S(1)}, u32[]{:S(2)}, u32[]{:S(2)}) async-start(f32[4,256,21]{1,2,0:T(8,128)} %broadcast_in_dim.22), calls=%async_computation.1 | async-start | bytes 196608 | tf_op jit(solution)/shard_map/all_to_all | solution.py:14
  90.4 1.1 reshape.133
  91.5 0.9 all-to-all-done.1
  94.2 4.0 %fusion.13 = (f32[256,2048]{1,0:T(8,128)S(1)}, f32[256,2048]{1,0:T(8,128)S(1)}) fusion(bf16[256,2048]{1,0:T(8,128)(2,1)S(1)} %copy-done.5, f32[256]{0:T(256)S(1)} %bitcast.156, f32[256]{0:T(256)S(1)} %bitcast.157, f32[256]{0:T(256)S(1)} %bitcast.158, f32[256]{0:T(256)S(1)} %bitcast.151, f32[256]{0:T(256)S(1)} %bitcast.161, bf16[256,4,2048]{2,0,1:T(8,128)(2,1)} %copy.82, ...), kind=kLoop, calls=%fused_computation.35 | loop fusion | flops 12058624 | bytes 9447424 | tf_op jit(solution)/shard_map/add | solution.py:85
  98.3 2.3 %fusion.21 = (f32[256,2048]{1,0:T(8,128)S(1)}, f32[256,2048]{1,0:T(8,128)S(1)}) fusion(bf16[256,2048]{1,0:T(8,128)(2,1)S(1)} %copy-done.5, f32[256]{0:T(256)S(1)} %bitcast.147, f32[256]{0:T(256)S(1)} %bitcast.148, f32[256]{0:T(256)S(1)} %bitcast.149, f32[256]{0:T(256)S(1)} %bitcast.150, f32[256]{0:T(256)S(1)} %bitcast.160, ...), kind=kLoop, calls=%fused_computation.43 | loop fusion | flops 12058624 | bytes 9447424 | tf_op jit(solution)/shard_map/add | solution.py:85
  100.6 0.9 multiply_reduce_fusion
  102.5 6.6 %fusion.29 = f32[256,24]{0,1:T(8,128)S(1)} fusion(f32[256,1,2048]{2,0,1:T(8,128)S(1)} %bitcast.129, f32[256,1,2048]{2,0,1:T(8,128)S(1)} %bitcast.126, f32[256,1,2048]{2,0,1:T(8,128)S(1)} %bitcast.123, f32[256,1,2048]{2,0,1:T(8,128)S(1)} %bitcast.120, f32[2048,24,4]{0,2,1:T(4,128)S(1)} %copy-done.6), kind=kOutput, calls=%fused_computation.55 | convolution fusion | flops 610271232 | bytes 9199616 | tf_op jit(solution)/shard_map/tic,kic->tk/dot_general | solution.py:119
  109.8 4.2 %all-to-all-start.2 = ((f32[4,256,25]{1,2,0:T(8,128)}), f32[4,256,25]{1,2,0:T(8,128)S(1)}, u32[]{:S(2)}, u32[]{:S(2)}) async-start(f32[4,256,25]{1,2,0:T(8,128)} %broadcast_in_dim.24), calls=%async_computation.2 | async-start | bytes 262144 | tf_op jit(solution)/shard_map/all_to_all | solution.py:14
  114.1 3.2 %fusion.27 = bf16[256,4,2048]{2,0,1:T(8,128)(2,1)S(1)} fusion(f32[256,1,2048]{2,0,1:T(8,128)} %bitcast.130, f32[256,1,2048]{2,0,1:T(8,128)} %bitcast.127, f32[256,1,2048]{2,0,1:T(8,128)} %bitcast.124, f32[256,1,2048]{2,0,1:T(8,128)S(1)} %bitcast.121), kind=kLoop, calls=%fused_computation.52 | loop fusion | flops 6291456 | bytes 12582912 | tf_op jit(solution)/shard_map/convert_element_type | solution.py:118
  117.3 5.3 %copy.90 = bf16[256,4,2048]{2,1,0:T(4,128)(2,1)} copy(bf16[256,4,2048]{2,0,1:T(8,128)(2,1)S(1)} %fusion.27) | data formatting | bytes 8388608
  122.6 1.3 fusion.49
  126.1 4.9 %multiply_reduce_fusion.1 = (f32[256]{0:T(256)S(1)}, f32[256,2048]{1,0:T(8,128)}) fusion(f32[256,2048]{1,0:T(8,128)} %copy-done.3, f32[256]{0:T(256)S(1)} %bitcast.164, f32[256,2048]{1,0:T(8,128)} %copy-done.2, f32[256]{0:T(256)S(1)} %bitcast.165, f32[256,2048]{1,0:T(8,128)} %copy-done.1, f32[256]{0:T(256)S(1)} %bitcast.166, ...), kind=kLoop, calls=%fused_computation.49 | loop fusion | flops 4718336 | bytes 10490880 | tf_op jit(solution)/shard_map/reduce_sum | solution.py:135
  131.6 3.5 %all-to-all-start.3 = ((f32[4,1,256]{2,1,0:T(1,128)}), f32[4,1,256]{2,1,0:T(1,128)S(1)}, u32[]{:S(2)}, u32[]{:S(2)}) async-start(f32[4,1,256]{2,1,0:T(1,128)} %broadcast_in_dim.25), calls=%async_computation.3 | async-start | bytes 8192 | tf_op jit(solution)/shard_map/all_to_all | solution.py:14
  135.7 2.5 %all-to-all-done.3 = f32[4,1,256]{2,1,0:T(1,128)S(1)} async-done(((f32[4,1,256]{2,1,0:T(1,128)}), f32[4,1,256]{2,1,0:T(1,128)S(1)}, u32[]{:S(2)}, u32[]{:S(2)}) %all-to-all-start.3) | async-done | bytes 4128 | tf_op jit(solution)/shard_map/all_to_all | solution.py:14
  138.2 2.9 %multiply_convert_fusion = bf16[256,2048]{1,0:T(8,128)(2,1)} fusion(f32[256,2048]{1,0:T(8,128)} %get-tuple-element.25, f32[2048]{0:T(1024)S(1)} %copy-done.9, f32[256]{0:T(256)S(1)} %add_sqrt_fusion), kind=kLoop, calls=%fused_computation.48 | loop fusion | flops 1572864 | bytes 3154944 | tf_op jit(solution)/shard_map/convert_element_type | solution.py:136
  (74 shorter events, 10.1 us)
Async XLA Ops:
  4.0 15.2 %copy-start.7 = (f32[44]{0:T(128)S(1)}, f32[44]{0:T(128)}, u32[]{:S(2)}) copy-start(f32[44]{0:T(128)} %param.11) | copy-start | bytes 532
  4.0 64.1 %all-to-all-start = ((f32[64,32,176]{2,1,0:T(8,128)}), f32[64,32,176]{2,1,0:T(8,128)S(1)}, u32[]{:S(2)}, u32[]{:S(2)}) async-start(f32[64,32,176]{2,1,0:T(8,128)} %stack.12), calls=%async_computation | async-start | bytes 4194304 | tf_op jit(solution)/shard_map/all_to_all | solution.py:27
  19.5 6.7 %copy-start.4 = (bf16[256,4,2048]{2,1,0:T(4,128)(2,1)S(1)}, bf16[256,4,2048]{2,1,0:T(4,128)(2,1)}, u32[]{:S(2)}) copy-start(bf16[256,4,2048]{2,1,0:T(4,128)(2,1)} %param.7) | copy-start | bytes 12582916
  70.7 18.4 %copy-start.8 = (f32[5]{0:T(128)S(1)}, f32[5]{0:T(128)}, u32[]{:S(2)}) copy-start(f32[5]{0:T(128)} %param.12) | copy-start | bytes 64
  81.0 11.4 %all-to-all-start.1 = ((f32[4,256,21]{1,2,0:T(8,128)}), f32[4,256,21]{1,2,0:T(8,128)S(1)}, u32[]{:S(2)}, u32[]{:S(2)}) async-start(f32[4,256,21]{1,2,0:T(8,128)} %broadcast_in_dim.22), calls=%async_computation.1 | async-start | bytes 196608 | tf_op jit(solution)/shard_map/all_to_all | solution.py:14
  90.4 3.9 %copy-start.5 = (bf16[256,2048]{1,0:T(8,128)(2,1)S(1)}, bf16[256,2048]{1,0:T(8,128)(2,1)}, u32[]{:S(2)}) copy-start(bf16[256,2048]{1,0:T(8,128)(2,1)} %param.8) | copy-start | bytes 3145732
  94.2 4.0 %copy-start = (bf16[256,4,2048]{2,0,1:T(8,128)(2,1)S(1)}, bf16[256,4,2048]{2,0,1:T(8,128)(2,1)}, u32[]{:S(2)}) copy-start(bf16[256,4,2048]{2,0,1:T(8,128)(2,1)} %copy.82) | copy-start | bytes 12582916
  98.2 3.2 %copy-start.1 = (f32[256,2048]{1,0:T(8,128)}, f32[256,2048]{1,0:T(8,128)S(1)}, u32[]{:S(2)}) copy-start(f32[256,2048]{1,0:T(8,128)S(1)} %get-tuple-element.29) | copy-start | bytes 6291460
  100.5 1.3 copy-start.2
  100.6 2.0 %copy-start.3 = (f32[256,2048]{1,0:T(8,128)}, f32[256,2048]{1,0:T(8,128)S(1)}, u32[]{:S(2)}) copy-start(f32[256,2048]{1,0:T(8,128)S(1)} %get-tuple-element.31) | copy-start | bytes 6291460
  100.6 2.0 %copy-start.6 = (f32[2048,24,4]{0,2,1:T(4,128)S(1)}, f32[2048,24,4]{0,2,1:T(4,128)}, u32[]{:S(2)}) copy-start(f32[2048,24,4]{0,2,1:T(4,128)} %reshape.133) | copy-start | bytes 2359300
  109.8 12.7 %all-to-all-start.2 = ((f32[4,256,25]{1,2,0:T(8,128)}), f32[4,256,25]{1,2,0:T(8,128)S(1)}, u32[]{:S(2)}, u32[]{:S(2)}) async-start(f32[4,256,25]{1,2,0:T(8,128)} %broadcast_in_dim.24), calls=%async_computation.2 | async-start | bytes 262144 | tf_op jit(solution)/shard_map/all_to_all | solution.py:14
  126.1 12.1 %copy-start.9 = (f32[2048]{0:T(1024)S(1)}, f32[2048]{0:T(1024)}, u32[]{:S(2)}) copy-start(f32[2048]{0:T(1024)} %param.13) | copy-start | bytes 24580
  131.6 6.6 %all-to-all-start.3 = ((f32[4,1,256]{2,1,0:T(1,128)}), f32[4,1,256]{2,1,0:T(1,128)S(1)}, u32[]{:S(2)}, u32[]{:S(2)}) async-start(f32[4,1,256]{2,1,0:T(1,128)} %broadcast_in_dim.25), calls=%async_computation.3 | async-start | bytes 8192 | tf_op jit(solution)/shard_map/all_to_all | solution.py:14
